TPU v7x, 512 devices: a whole 4x4x16 slice. The times are simulated.
512 devices in a mesh: ep: 64 (over x_lo, z, core), blk: 8 (over x_hi, y).
Axes of the slice: x: 4 (x_hi: 2, x_lo: 2; x = x_hi * 2 + x_lo), y: 4, z: 16, core: 2. Of those that a mesh axis runs over, the one named last changes fastest.
Arguments:
- tokens: bfloat16 [4096, 2048], P(('ep', 'blk')), may hold values from -6 to 6
- routes: int32 [4096, 8], P('ep'), may hold values from 0 to 63, all different within a row; in each aligned block of 64 rows (0 to 63, 64 to 127, ...) at most 16 rows name the same one
- gate_scale: bfloat16 [4096, 8], P('ep'), may hold values from 0.099609375 to 1
- placement: int32 [64], replicated, may hold values from 0 to 63, each once
- w_gate: bfloat16 [64, 2048, 1024], P('ep', None, 'blk'), may hold values from -0.125 to 0.125
- w_up: bfloat16 [64, 2048, 1024], P('ep', None, 'blk'), may hold values from -0.125 to 0.125
- w_down: bfloat16 [64, 1024, 2048], P('ep', 'blk'), may hold values from -0.1875 to 0.1875
Outputs:
- mixed: bfloat16 [4096, 2048], P(('ep', 'blk'))
Inputs may be any that keep to these rules, and one draw needn't show every extreme that they name: `routes`: in each aligned block of 64 rows (the tokens of one index of ep) no expert is named by more than 16 rows, a bound that some block reaches; a row names 8 different experts. `placement`: each ep index holds exactly one expert.
All inputs are finite; a program needn't handle non-finite values.
Results may differ from a plain program's by a relative error of at most 0.019.
Values may be sent and summed in bfloat16 or wider, within the bound.
A program may use at most 64 MiB of HBM per device.

v0:
```python
import jax
import jax.numpy as jnp
from jax import lax
from jax.sharding import PartitionSpec as P

TOP = 8


def expert_rows(arrived, w_gate, w_up, w_down):
    row_shape = arrived.shape
    flat_rows = arrived.reshape(-1, row_shape[-1])
    gate_proj = jnp.dot(flat_rows, w_gate[0], preferred_element_type=jnp.float32)
    up_proj = jnp.dot(flat_rows, w_up[0], preferred_element_type=jnp.float32)
    hidden = (jax.nn.silu(gate_proj) * up_proj).astype(jnp.bfloat16)
    output = jnp.dot(hidden, w_down[0], preferred_element_type=jnp.float32).astype(jnp.bfloat16)
    return output.reshape(row_shape)


def local(tokens, routes, gate_scale, placement, w_gate, w_up, w_down):
    ep_count = lax.axis_size("ep")
    blk_count = lax.axis_size("blk")
    own_count = tokens.shape[0]
    width = tokens.shape[1]
    block_size = own_count * blk_count
    capacity = blk_count * max(1, 2 * TOP * own_count // ep_count)
    slots_total = ep_count * capacity
    gathered = lax.all_gather(tokens, "blk", axis=0, tiled=True)
    ep_ids = lax.iota(jnp.int32, ep_count)
    holder = jnp.sum(
        jnp.where(routes[:, :, None] == ep_ids[None, None, :], placement[None, None, :], 0), axis=-1
    )
    flat_holder = holder.reshape(-1)
    onehot = (flat_holder[:, None] == ep_ids[None, :]).astype(jnp.int32)
    before = jnp.cumsum(onehot, axis=0) - onehot
    slot_index = jnp.sum(before * onehot, axis=1)
    position = flat_holder * capacity + slot_index
    matches = (position[None, :] == lax.iota(jnp.int32, slots_total)[:, None]).reshape(
        slots_total, block_size, TOP
    )
    picked = jnp.any(matches, axis=2).astype(jnp.bfloat16)
    buffer = jnp.dot(picked, gathered, preferred_element_type=jnp.float32).astype(jnp.bfloat16)
    buffer = buffer.reshape(ep_count, capacity, width)
    combine_weights = jnp.sum(
        jnp.where(matches, gate_scale[None, :, :], jnp.zeros((), jnp.bfloat16)), axis=2
    )
    finished = None
    arrived = lax.all_to_all(buffer, "ep", split_axis=0, concat_axis=0, tiled=True)
    returned = lax.all_to_all(
        expert_rows(arrived, w_gate, w_up, w_down), "ep", split_axis=0, concat_axis=0, tiled=True
    )
    returned_flat = returned.reshape(slots_total, width)
    combined = lax.dot_general(
        combine_weights, returned_flat, (((0,), (0,)), ((), ())), preferred_element_type=jnp.float32
    )
    summed = lax.psum_scatter(combined.astype(jnp.bfloat16), "blk", scatter_dimension=0, tiled=True)
    finished = summed
    return finished


def solution(mesh):
    in_specs = (
        P(("ep", "blk"), None),
        P("ep", None),
        P("ep", None),
        P(),
        P("ep", None, "blk"),
        P("ep", None, "blk"),
        P("ep", "blk", None),
    )
    out_specs = P(("ep", "blk"), None)
    return jax.shard_map(local, mesh=mesh, in_specs=in_specs, out_specs=out_specs, check_vma=False)
```

profile of v0, /device:TPU:32, one launch (start us, length us, event | category | flops | bytes accessed | tf_op | source)
XLA Modules:
  0.0 550.5 jit_solution(13190970564214001270)
XLA Ops:
  6.5 0.0 copy-start
  6.5 0.8 copy.13
  7.4 1.9 select_reduce_fusion
  9.3 0.1 eq.59
  9.4 0.1 eq.55
  9.5 1.2 reduce-window.6
  10.7 0.2 slice_reduce_fusion
  10.9 0.1 fusion.17
  11.1 0.1 reduce_sum.34
  11.2 0.7 fusion
  11.9 35.2 %all_gather.3 = bf16[64,2048]{1,0:T(8,128)(2,1)S(1)} all-gather(bf16[8,2048]{1,0:T(8,128)(2,1)} %param.7), channel_id=1, replica_groups=mesh['ep'=64,'blk'=8] {'blk'}, dimensions={0}, use_global_device_ids=true | all-gather | bytes 294912 | tf_op jit(solution)/shard_map/all_gather | solution.py:27
  47.1 1.3 convolution_convert_fusion.1
  48.4 0.0 copy-start.2
  48.5 202.3 %all_to_all.10 = bf16[64,16,2048]{2,1,0:T(8,128)(2,1)S(1)} all-to-all(bf16[64,16,2048]{2,1,0:T(8,128)(2,1)S(1)} %bitcast.42), channel_id=1, replica_groups=mesh['ep'=64,'blk'=8] {'ep'}, dimensions={0} | all-to-all | bytes 8388608 | tf_op jit(solution)/shard_map/all_to_all | solution.py:47
  250.8 0.0 copy-start.1
  250.8 0.0 copy-start.3
  250.8 1.9 copy-done.1
  252.7 0.0 copy-done.2
  252.7 1.2 fusion.7
  254.0 0.0 copy-done
  254.0 0.0 copy-done.3
  254.0 8.5 %convolution_convert_fusion = bf16[1024,2048]{1,0:T(8,128)(2,1)} fusion(bf16[1024,2048]{1,0:T(8,128)(2,1)} %bitcast.40, bf16[1,128,2048]{2,1,0:T(8,128)(2,1)S(1)} %copy-done, bf16[1,2048,128]{2,1,0:T(8,128)(2,1)S(1)} %copy-done.3, f32[1024,128]{1,0:T(8,128)S(1)} %fusion.7), kind=kOutput, calls=%fused_computation | convolution fusion | flops 1076625408 | bytes 9961472 | tf_op jit(solution)/shard_map/dot_general | solution.py:15
  262.5 0.0 copy-start.4
  262.5 8.8 %all-to-all-start.1 = ((bf16[64,16,2048]{2,1,0:T(8,128)(2,1)}), bf16[64,16,2048]{2,1,0:T(8,128)(2,1)}, u32[]{:S(2)}, u32[]{:S(2)}) async-start(bf16[64,16,2048]{2,1,0:T(8,128)(2,1)} %bitcast.41), calls=%async_computation.1 | async-start | bytes 8388608 | tf_op jit(solution)/shard_map/all_to_all | solution.py:48
  271.3 0.0 reduce-scatter.2.cloned.1.call-start
  271.3 0.0 copy-done.4
  271.3 0.1 copy.15
  271.4 0.7 fusion.3
  272.2 183.0 %all-to-all-done.1 = bf16[64,16,2048]{2,1,0:T(8,128)(2,1)} async-done(((bf16[64,16,2048]{2,1,0:T(8,128)(2,1)}), bf16[64,16,2048]{2,1,0:T(8,128)(2,1)}, u32[]{:S(2)}, u32[]{:S(2)}) %all-to-all-start.1) | async-done | bytes 4194336 | tf_op jit(solution)/shard_map/all_to_all | solution.py:48
  455.2 3.7 convolution_convert_fusion.2
  458.9 0.0 reduce-scatter.2.cloned.1.call-update
  458.9 84.7 %reduce-scatter.2.cloned.1.call-done = bf16[8,2048]{1,0:T(8,128)(2,1)} async-done(((bf16[64,2048]{1,0:T(8,128)(2,1)}), bf16[8,2048]{1,0:T(8,128)(2,1)}) %reduce-scatter.2.cloned.1.call-update) | async-done | bytes 32784 | tf_op jit(solution)/shard_map/reduce_scatter | solution.py:55
  (4 shorter events, 0.1 us)
Async XLA Ops:
  6.5 247.4 %copy-start = (bf16[1,128,2048]{2,1,0:T(8,128)(2,1)S(1)}, bf16[1,128,2048]{2,1,0:T(8,128)(2,1)}, u32[]{:S(2)}) copy-start(bf16[1,128,2048]{2,1,0:T(8,128)(2,1)} %param.13) | copy-start | bytes 1572868
  48.4 204.3 %copy-start.2 = (bf16[1,2048,128]{2,1,0:T(8,128)(2,1)S(1)}, bf16[1,2048,128]{2,1,0:T(8,128)(2,1)}, u32[]{:S(2)}) copy-start(bf16[1,2048,128]{2,1,0:T(8,128)(2,1)} %param.11) | copy-start | bytes 1572868
  250.8 1.9 copy-start.1
  250.8 3.2 copy-start.3
  262.5 8.8 %copy-start.4 = (bf16[64,8]{0,1:T(8,128)(2,1)S(1)}, bf16[64,8]{0,1:T(8,128)(2,1)}, u32[]{:S(2)}) copy-start(bf16[64,8]{0,1:T(8,128)(2,1)} %param.9) | copy-start | bytes 3076
  262.5 192.7 %all-to-all-start.1 = ((bf16[64,16,2048]{2,1,0:T(8,128)(2,1)}), bf16[64,16,2048]{2,1,0:T(8,128)(2,1)}, u32[]{:S(2)}, u32[]{:S(2)}) async-start(bf16[64,16,2048]{2,1,0:T(8,128)(2,1)} %bitcast.41), calls=%async_computation.1 | async-start | bytes 8388608 | tf_op jit(solution)/shard_map/all_to_all | solution.py:48
  271.3 272.4 %reduce-scatter.2.cloned.1.call-start = ((), (), s32[]{:S(2)}) async-start(), calls=%async_computation.3 | async-start | bytes 294912 | tf_op jit(solution)/shard_map/reduce_scatter | solution.py:55
Sparse Core Ops, SparseCore 0:
  459.1 84.5 reduce-scatter.1
where the time goes:
time: 551 us
  waiting for transfers between devices  268 us (49%)
  blocking collectives  238 us (43%)
  matrix products  14.8 us (3%)
  between operations  13.5 us (2%)
  starting transfers between devices  8.82 us (2%)
    all_to_all x1, blocking collectives, local(): lax.all_to_all(buffer, 'ep', split_axis=0, concat_axis=0, tiled=True)  202 us
    all_to_all x1, waiting for transfers between devices, local(): lax.all_to_all(expert_rows(arrived, w_gate, w_up, w_down), 'ep', split_ax...  183 us
    reduce_scatter x1, waiting for transfers between devices, local(): lax.psum_scatter(combined.astype(jnp.bfloat16), 'blk', scatter_dimension=...  84.7 us
    all_gather x1, blocking collectives, local(): gathered = lax.all_gather(tokens, 'blk', axis=0, tiled=True)  35.2 us
  transfers between devices with their start and end apart: 2, of which 2 were waited for; matrix products, arithmetic and copies ran while one was open for 0% of the time, Pallas kernels for 0%

commit v1 on v0

--- a/solution.py
+++ b/solution.py
@@ -24,7 +24,9 @@
     block_size = own_count * blk_count
     capacity = blk_count * max(1, 2 * TOP * own_count // ep_count)
     slots_total = ep_count * capacity
-    gathered = lax.all_gather(tokens, "blk", axis=0, tiled=True)
+    gathered = jnp.concatenate(
+        lax.all_to_all(jnp.stack([tokens for _ in range(lax.axis_size("blk"))]), "blk", 0, 0), 0
+    )
     ep_ids = lax.iota(jnp.int32, ep_count)
     holder = jnp.sum(
         jnp.where(routes[:, :, None] == ep_ids[None, None, :], placement[None, None, :], 0), axis=-1

time: 551 us -> 525 us (0.953)
  blocking collectives: 238 us -> 202 us
  starting transfers between devices: 8.82 us -> 15.8 us
    all_gather x1 -> x0, blocking collectives: 35.2 us -> none  [local(): gathered = lax.all_gather(tokens, 'blk', axis=0, tiled=True)]
    all_to_all x0 -> x1, starting transfers between devices: none -> 6.93 us  [local(): lax.all_to_all(jnp.stack([tokens for _ in range(lax.axis_size('blk'))]),...]
  transfers between devices with their start and end apart: 2 -> 3, of which waited for: 2 -> 3; matrix products, arithmetic and copies ran while one was open for 0% -> 1% of each run, Pallas kernels for 0% -> 0%
where the time goes in v1:
time: 525 us
  waiting for transfers between devices  269 us (51%)
  blocking collectives  202 us (38%)
  starting transfers between devices  15.8 us (3%)
  matrix products  14.8 us (3%)
  between operations  13.5 us (3%)
    all_to_all x1, blocking collectives, local(): lax.all_to_all(buffer, 'ep', split_axis=0, concat_axis=0, tiled=True)  202 us
    all_to_all x1, waiting for transfers between devices, local(): lax.all_to_all(expert_rows(arrived, w_gate, w_up, w_down), 'ep', split_ax...  183 us
    reduce_scatter x1, waiting for transfers between devices, local(): lax.psum_scatter(combined.astype(jnp.bfloat16), 'blk', scatter_dimension=...  82.6 us
  transfers between devices with their start and end apart: 3, of which 3 were waited for; matrix products, arithmetic and copies ran while one was open for 1% of the time, Pallas kernels for 0%

profile of v1, /device:TPU:32, one launch (start us, length us, event | category | flops | bytes accessed | tf_op | source)
XLA Modules:
  0.0 524.7 jit_solution(7216064501042902869)
XLA Ops:
  6.5 0.0 copy-start
  6.5 1.5 stack.2
  8.1 6.9 %all-to-all-start = ((bf16[8,8,2048]{2,1,0:T(8,128)(2,1)}), bf16[8,8,2048]{2,1,0:T(8,128)(2,1)S(1)}, u32[]{:S(2)}, u32[]{:S(2)}) async-start(bf16[8,8,2048]{2,1,0:T(8,128)(2,1)} %stack.2), calls=%async_computation | async-start | bytes 524288 | tf_op jit(solution)/shard_map/all_to_all | solution.py:28
  15.0 0.8 copy.13
  15.8 1.9 select_reduce_fusion
  17.7 0.1 eq.59
  17.8 0.1 eq.55
  17.9 1.2 reduce-window.6
  19.1 0.2 slice_reduce_fusion
  19.3 0.1 fusion.18
  19.5 0.1 reduce_sum.34
  19.6 0.7 fusion
  20.3 3.4 all-to-all-done
  23.7 1.3 convolution_convert_fusion.1
  25.0 0.0 copy-start.2
  25.0 202.0 %all_to_all.15 = bf16[64,16,2048]{2,1,0:T(8,128)(2,1)S(1)} all-to-all(bf16[64,16,2048]{2,1,0:T(8,128)(2,1)S(1)} %bitcast.44), channel_id=1, replica_groups=mesh['ep'=64,'blk'=8] {'ep'}, dimensions={0} | all-to-all | bytes 8388608 | tf_op jit(solution)/shard_map/all_to_all | solution.py:49
  227.1 0.0 copy-start.1
  227.1 0.0 copy-start.3
  227.1 1.9 copy-done.1
  229.0 0.0 copy-done.2
  229.0 1.2 fusion.7
  230.3 0.0 copy-done
  230.3 0.0 copy-done.3
  230.3 8.5 %convolution_convert_fusion = bf16[1024,2048]{1,0:T(8,128)(2,1)} fusion(bf16[1024,2048]{1,0:T(8,128)(2,1)} %bitcast.42, bf16[1,128,2048]{2,1,0:T(8,128)(2,1)S(1)} %copy-done, bf16[1,2048,128]{2,1,0:T(8,128)(2,1)S(1)} %copy-done.3, f32[1024,128]{1,0:T(8,128)S(1)} %fusion.7), kind=kOutput, calls=%fused_computation | convolution fusion | flops 1076625408 | bytes 9961472 | tf_op jit(solution)/shard_map/dot_general | solution.py:15
  238.8 0.0 copy-start.4
  238.8 8.8 %all-to-all-start.2 = ((bf16[64,16,2048]{2,1,0:T(8,128)(2,1)}), bf16[64,16,2048]{2,1,0:T(8,128)(2,1)}, u32[]{:S(2)}, u32[]{:S(2)}) async-start(bf16[64,16,2048]{2,1,0:T(8,128)(2,1)} %bitcast.43), calls=%async_computation.2 | async-start | bytes 8388608 | tf_op jit(solution)/shard_map/all_to_all | solution.py:50
  247.6 0.0 reduce-scatter.2.cloned.1.call-start
  247.6 0.0 copy-done.4
  247.6 0.1 copy.15
  247.7 0.7 fusion.3
  248.5 183.0 %all-to-all-done.2 = bf16[64,16,2048]{2,1,0:T(8,128)(2,1)} async-done(((bf16[64,16,2048]{2,1,0:T(8,128)(2,1)}), bf16[64,16,2048]{2,1,0:T(8,128)(2,1)}, u32[]{:S(2)}, u32[]{:S(2)}) %all-to-all-start.2) | async-done | bytes 4194336 | tf_op jit(solution)/shard_map/all_to_all | solution.py:50
  431.5 3.7 convolution_convert_fusion.2
  435.2 0.0 reduce-scatter.2.cloned.1.call-update
  435.3 82.6 %reduce-scatter.2.cloned.1.call-done = bf16[8,2048]{1,0:T(8,128)(2,1)} async-done(((bf16[64,2048]{1,0:T(8,128)(2,1)}), bf16[8,2048]{1,0:T(8,128)(2,1)}) %reduce-scatter.2.cloned.1.call-update) | async-done | bytes 32784 | tf_op jit(solution)/shard_map/reduce_scatter | solution.py:57
  (4 shorter events, 0.1 us)
Async XLA Ops:
  6.5 223.7 %copy-start = (bf16[1,128,2048]{2,1,0:T(8,128)(2,1)S(1)}, bf16[1,128,2048]{2,1,0:T(8,128)(2,1)}, u32[]{:S(2)}) copy-start(bf16[1,128,2048]{2,1,0:T(8,128)(2,1)} %param.13) | copy-start | bytes 1572868
  8.1 15.7 %all-to-all-start = ((bf16[8,8,2048]{2,1,0:T(8,128)(2,1)}), bf16[8,8,2048]{2,1,0:T(8,128)(2,1)S(1)}, u32[]{:S(2)}, u32[]{:S(2)}) async-start(bf16[8,8,2048]{2,1,0:T(8,128)(2,1)} %stack.2), calls=%async_computation | async-start | bytes 524288 | tf_op jit(solution)/shard_map/all_to_all | solution.py:28
  25.0 204.0 %copy-start.2 = (bf16[1,2048,128]{2,1,0:T(8,128)(2,1)S(1)}, bf16[1,2048,128]{2,1,0:T(8,128)(2,1)}, u32[]{:S(2)}) copy-start(bf16[1,2048,128]{2,1,0:T(8,128)(2,1)} %param.11) | copy-start | bytes 1572868
  227.1 1.9 copy-start.1
  227.1 3.2 copy-start.3
  238.8 8.8 %copy-start.4 = (bf16[64,8]{0,1:T(8,128)(2,1)S(1)}, bf16[64,8]{0,1:T(8,128)(2,1)}, u32[]{:S(2)}) copy-start(bf16[64,8]{0,1:T(8,128)(2,1)} %param.9) | copy-start | bytes 3076
  238.8 192.7 %all-to-all-start.2 = ((bf16[64,16,2048]{2,1,0:T(8,128)(2,1)}), bf16[64,16,2048]{2,1,0:T(8,128)(2,1)}, u32[]{:S(2)}, u32[]{:S(2)}) async-start(bf16[64,16,2048]{2,1,0:T(8,128)(2,1)} %bitcast.43), calls=%async_computation.2 | async-start | bytes 8388608 | tf_op jit(solution)/shard_map/all_to_all | solution.py:50
  247.6 270.3 %reduce-scatter.2.cloned.1.call-start = ((), (), s32[]{:S(2)}) async-start(), calls=%async_computation.4 | async-start | bytes 294912 | tf_op jit(solution)/shard_map/reduce_scatter | solution.py:57
Sparse Core Ops, SparseCore 0:
  435.4 82.4 reduce-scatter.1
